TPU v7x, 256 devices: a whole 4x4x8 slice. The times are simulated.
256 devices in a mesh: gx: 16 (over y_lo, z), gy: 16 (over y_hi, x, core).
Axes of the slice: x: 4, y: 4 (y_hi: 2, y_lo: 2; y = y_hi * 2 + y_lo), z: 8, core: 2. Of those that a mesh axis runs over, the one named last changes fastest.
Arguments:
- adjoint_in: float32 [57, 4, 128, 2048], P(None, None, 'gx', 'gy'), may hold values from -6 to 6
- populations_early: bfloat16 [57, 4, 128, 2048], P(None, None, 'gx', 'gy'), may hold values from 0.019897461 to 0.099609375
- populations_late: bfloat16 [57, 4, 128, 2048], P(None, None, 'gx', 'gy'), may hold values from 0.019897461 to 0.099609375
- dipoles_early: bfloat16 [3, 4, 128, 2048], P(None, None, 'gx', 'gy'), may hold values from -4 to 4
- dipoles_late: bfloat16 [3, 4, 128, 2048], P(None, None, 'gx', 'gy'), may hold values from -4 to 4
Outputs:
- adjoint_out: float32 [57, 4, 128, 2048], P(None, None, 'gx', 'gy')
All inputs are finite; a program needn't handle non-finite values.
Results may differ from a plain program's by a relative error of at most 0.0003.
Values sent between devices are 32-bit elements; how exact they have to be, the bound alone decides.
A program may use at most 128 MiB of HBM per device.

v0:
```python
import jax
import jax.numpy as jnp
from jax import lax
from jax.experimental import pallas as pl
from jax.experimental.pallas import tpu as pltpu
from jax.sharding import PartitionSpec as P

MESH = pl.DeviceIdType.MESH
VELOCITY = (
    (1, 0, 0),
    (-1, 0, 0),
    (0, 1, 0),
    (0, -1, 0),
    (1, 1, 0),
    (-1, -1, 0),
    (1, -1, 0),
    (-1, 1, 0),
    (1, 0, 1),
    (-1, 0, -1),
    (1, 0, -1),
    (-1, 0, 1),
    (0, 1, 1),
    (0, -1, -1),
    (0, 1, -1),
    (0, -1, 1),
    (0, 0, 0),
    (0, 0, 1),
    (0, 0, -1),
)
TAU = (1.0, 1.0, 1.25)
G = ((0.0, 1.2, -0.6), (1.2, 0.0, -0.6), (-0.6, -0.6, -0.3))
ORDER = (1, 5, 7, 9, 11, 2, 3, 12, 13, 14, 15, 16, 17, 18, 0, 4, 6, 8, 10)
SLOT = {q: i for i, q in enumerate(ORDER)}
F32 = jnp.float32


def up_y(v):
    return pltpu.roll(v, 127, 1)


def dn_y(v):
    return pltpu.roll(v, 1, 1)


def shift_y(v, cy):
    return v if cy == 0 else (up_y(v) if cy == 1 else dn_y(v))


def near(ld, f):
    n = dict(
        c=ld(f, 0, 0),
        xp=ld(f, 1, 0),
        xm=ld(f, -1, 0),
        zp=ld(f, 0, 1),
        zm=ld(f, 0, -1),
        pp=ld(f, 1, 1),
        pm=ld(f, 1, -1),
        mp=ld(f, -1, 1),
        mm=ld(f, -1, -1),
    )
    n["dx"] = n["xp"] - n["xm"]
    n["dz"] = n["zp"] - n["zm"]
    n["sx"] = n["xp"] + n["xm"]
    n["sz"] = n["zp"] + n["zm"]
    return n


def corner(n):
    return (n["pp"] + n["mm"]) + (n["pm"] + n["mp"])


def cross(n):
    return (n["pp"] + n["mm"]) - (n["pm"] + n["mp"])


def corner_x(n):
    return (n["pp"] - n["mm"]) + (n["pm"] - n["mp"])


def corner_z(n):
    return (n["pp"] - n["mm"]) - (n["pm"] - n["mp"])


def gradient(n):
    h = 2.0 * n["c"] + n["sx"] + n["sz"]
    r = dict(
        hp=up_y(h),
        hm=dn_y(h),
        dxp=up_y(n["dx"]),
        dxm=dn_y(n["dx"]),
        dzp=up_y(n["dz"]),
        dzm=dn_y(n["dz"]),
    )
    gx = 2.0 * n["dx"] + corner_x(n) + (r["dxp"] + r["dxm"])
    gz = 2.0 * n["dz"] + corner_z(n) + (r["dzp"] + r["dzm"])
    return (gx, r["hp"] - r["hm"], gz), r


def second(sx, sz, cor, crs, r):
    xx = 2.0 * sx + cor + (up_y(sx) + dn_y(sx))
    zz = 2.0 * sz + cor + (up_y(sz) + dn_y(sz))
    return dict(
        xx=xx,
        yy=r["hp"] + r["hm"],
        zz=zz,
        xy=r["dxp"] - r["dxm"],
        yz=r["dzp"] - r["dzm"],
        xz=crs,
    )


def vector_stencil(nx, ny, nz):
    px = 2.0 * nx["sx"] + corner(nx) + cross(nz)
    px = px + up_y(nx["sx"] + ny["dx"]) + dn_y(nx["sx"] - ny["dx"])
    pz = 2.0 * nz["sz"] + corner(nz) + cross(nx)
    pz = pz + up_y(nz["sz"] + ny["dz"]) + dn_y(nz["sz"] - ny["dz"])
    a = 2.0 * ny["c"] + ny["sx"] + ny["sz"]
    b = nx["dx"] + nz["dz"]
    return px, up_y(a + b) + dn_y(a - b), pz


def divergence(nx, ny, nz):
    u = nx["dx"] + nz["dz"]
    v = 2.0 * ny["c"] + ny["sx"] + ny["sz"]
    return 2.0 * u + corner_x(nx) + corner_z(nz) + up_y(u + v) + dn_y(u - v)


def moments_of(g):
    p = {}
    m = {}
    for q in (0, 2, 4, 6, 8, 10, 12, 14, 17):
        p[q] = g[q] + g[q + 1]
        m[q] = g[q] - g[q + 1]
    xy, xz, yz = p[4] + p[6], p[8] + p[10], p[12] + p[14]
    ax, ay, az = 2.0 * p[0], 2.0 * p[2], 2.0 * p[17]
    a = 12.0 * g[16] + (ax + ay + az) + (xy + xz + yz)
    b = (
        2.0 * m[0] + (m[4] + m[6]) + (m[8] + m[10]),
        2.0 * m[2] + (m[4] - m[6]) + (m[12] + m[14]),
        2.0 * m[17] + (m[8] - m[10]) + (m[12] - m[14]),
    )
    c = dict(
        xx=ax + xy + xz,
        yy=ay + xy + yz,
        zz=az + xz + yz,
        xy=p[4] - p[6],
        xz=p[8] - p[10],
        yz=p[12] - p[14],
    )
    return a, b, c


def pick_potentials(rho, d):
    psi = [1.0 - jnp.exp(-r) for r in rho]
    mixed = [
        1.2 * psi[1] - 0.6 * psi[2],
        1.2 * psi[0] - 0.6 * psi[2],
        -0.6 * (psi[0] + psi[1]) - 0.3 * psi[2],
    ]
    return psi, mixed + [d[j] * psi[2] for j in range(3)]


def thrusts(ld, d):
    grads, rolled, sums = [], [], []
    for s in range(3):
        n = near(ld, s)
        g, r = gradient(n)
        grads.append(g)
        if s < 2:
            rolled.append(r)
            sums.append((n["sx"], n["sz"], corner(n), cross(n)))
    diff = [b - a for a, b in zip(*sums)]
    r = {key: rolled[1][key] - rolled[0][key] for key in rolled[0]}
    m = second(*diff, r)
    e = [near(ld, 3 + j) for j in range(3)]
    p = vector_stencil(*e)
    k = 1.0 / 36.0
    k2 = 1.0 / (36.0 * 1.2)
    turned = (
        m["xx"] * d[0] + m["xy"] * d[1] + m["xz"] * d[2],
        m["xy"] * d[0] + m["yy"] * d[1] + m["yz"] * d[2],
        m["xz"] * d[0] + m["yz"] * d[1] + m["zz"] * d[2],
    )
    t0 = [-k * (grads[0][i] + p[i]) for i in range(3)]
    t1 = [k * (p[i] - grads[1][i]) for i in range(3)]
    t2 = [k2 * turned[i] - k * grads[2][i] for i in range(3)]
    return t0 + t1 + t2


def local_adjoint(mom, rho, u, psi, t, d):
    x, e_val, wt, ratio = [], [], [], []
    m = [None] * 3
    for s in range(3):
        a, b, c = mom[s]
        ratio.append(TAU[s] * psi[s] / rho[s])
        ts = t[3 * s : 3 * s + 3]
        v = [u[i] + ratio[s] * ts[i] for i in range(3)]
        cv = (
            c["xx"] * v[0] + c["xy"] * v[1] + c["xz"] * v[2],
            c["xy"] * v[0] + c["yy"] * v[1] + c["yz"] * v[2],
            c["xz"] * v[0] + c["yz"] * v[1] + c["zz"] * v[2],
        )
        k = 1.0 / (36.0 * TAU[s])
        b3 = [3.0 * b[i] for i in range(3)]
        a3 = 3.0 * a
        w = [b3[i] + 9.0 * cv[i] - a3 * v[i] for i in range(3)]
        half = (b3[0] + w[0]) * v[0] + (b3[1] + w[1]) * v[1] + (b3[2] + w[2]) * v[2]
        e_val.append(k * a + (0.5 * k) * half)
        w = [k * w[i] for i in range(3)]
        wt.append(w[0] * ts[0] + w[1] * ts[1] + w[2] * ts[2])
        for i in range(3):
            term = rho[s] * w[i]
            m[i] = term if s == 0 else m[i] + term
        tp = TAU[s] * psi[s]
        x.extend(tp * w[i] for i in range(3))
    inverse = 1.0 / (rho[0] + rho[1] + rho[2])
    m = [m[i] * inverse for i in range(3)]
    mu = m[0] * u[0] + m[1] * u[1] + m[2] * u[2]
    dens = [e_val[s] + wt[s] * (TAU[s] * (1.0 - psi[s]) - ratio[s]) - mu for s in range(3)]
    y = x[6:9]
    kxx, kyy, kzz = y[0] * d[0], y[1] * d[1], y[2] * d[2]
    kept = [
        kxx,
        kyy,
        kzz,
        y[0] * d[1] + y[1] * d[0],
        y[0] * d[2] + y[2] * d[0],
        y[1] * d[2] + y[2] * d[1],
        kxx + kyy,
        kyy + kzz,
        kxx + kzz,
    ]
    return x + kept, m, dens


def spread(ld, dens, psi, d):
    n = [[near(ld, 3 * s + i) for i in range(3)] for s in range(3)]
    y = [divergence(*n[s]) for s in range(3)]
    diff = [{key: n[0][i][key] - n[1][i][key] for key in n[0][i]} for i in range(3)]
    z = vector_stencil(*diff)
    xx, zz, a3, kxz = near(ld, 9), near(ld, 11), near(ld, 17), near(ld, 13)
    a1, a2, kxy, kyz = near(ld, 15), near(ld, 16), near(ld, 12), near(ld, 14)
    u = 2.0 * ld(10, 0, 0) + a1["sx"] + a2["sz"]
    v = kxy["dx"] + kyz["dz"]
    quad = 2.0 * (xx["sx"] + zz["sz"]) + corner(a3) + cross(kxz) + up_y(u + v) + dn_y(u - v)
    k = 1.0 / 36.0
    back = [
        1.2 * y[1] - 0.6 * y[2] + quad,
        1.2 * y[0] - 0.6 * y[2] - quad,
        -0.6 * (y[0] + y[1]) - 0.3 * y[2] - (d[0] * z[0] + d[1] * z[1] + d[2] * z[2]),
    ]
    return [dens[s] + (k * (1.0 - psi[s])) * back[s] for s in range(3)]


def late_moments(ld, pulled):
    x, y, z = (near(ld, i) for i in range(3))
    axx, azz = 2.0 * x["dx"], 2.0 * z["dz"]
    ayy = 2.0 * (up_y(y["c"]) - dn_y(y["c"]))
    exz = corner_x(x) + corner_z(z)
    exy = up_y(x["dx"] + y["sx"]) + dn_y(x["dx"] - y["sx"])
    eyz = up_y(z["dz"] + y["sz"]) + dn_y(z["dz"] - y["sz"])
    a_m = (axx + ayy + azz) + (exy + exz + eyz)
    b_m = vector_stencil(x, y, z)
    c_m = dict(
        xx=axx + exy + exz,
        yy=ayy + exy + eyz,
        zz=azz + exz + eyz,
        xy=up_y(y["dx"] + x["sx"]) + dn_y(y["dx"] - x["sx"]),
        yz=up_y(y["dz"] + z["sz"]) + dn_y(y["dz"] - z["sz"]),
        xz=corner_z(x) + corner_x(z),
    )
    extra = moments_of(pulled)
    out = []
    for s in range(3):
        n = near(ld, 3 + s)
        g, r = gradient(n)
        c = second(n["sx"], n["sz"], corner(n), cross(n), r)
        a = 12.0 * n["c"] + 2.0 * (n["sx"] + n["sz"]) + corner(n) + c["yy"] + a_m
        b = [g[i] + b_m[i] for i in range(3)]
        c = {key: c[key] + c_m[key] for key in c}
        if s == 2:
            a = a + 0.2 * extra[0]
            b = [b[i] + 0.2 * extra[1][i] for i in range(3)]
            c = {key: c[key] + 0.2 * extra[2][key] for key in c}
        out.append((a, b, c))
    return out


def kernel(
    size_x,
    size_y,
    a_in,
    pe_in,
    pl_in,
    de_in,
    dl_in,
    o_out,
    A,
    NE,
    NL,
    DE,
    DL,
    OUT,
    F,
    FL,
    FE,
    FM,
    FG,
    PO,
    PLX,
    PRX,
    PGO,
    PGL,
    PGR,
    PMO,
    PML,
    PMR,
    SA,
    SG,
    SL,
    SE,
    QM,
    QS,
    TB,
    SI,
    XM,
    XS,
    LM,
    LS,
    MS,
    TS,
    lsem,
    ssem,
    rsem,
):
    gx, gy = lax.axis_index("gx"), lax.axis_index("gy")
    xu, xd = lax.rem(gx + 1, size_x), lax.rem(gx + size_x - 1, size_x)
    yr, yl = lax.rem(gy + 1, size_y), lax.rem(gy + size_y - 1, size_y)
    everyone = [(xu, gy), (xd, gy), (gx, yr), (gx, yl), (xu, yr), (xu, yl), (xd, yr), (xd, yl)]
    barrier = pltpu.get_barrier_semaphore()
    for who in everyone:
        pl.semaphore_signal(barrier, inc=1, device_id=who, device_id_type=MESH)
    loads = [
        pltpu.make_async_copy(src, dst, lsem.at[i])
        for i, (src, dst) in enumerate(
            ((pl_in, NL), (dl_in, DL), (a_in, A), (pe_in, NE), (de_in, DE))
        )
    ]
    for copy in loads:
        copy.start()

    lane = lax.broadcasted_iota(jnp.int32, (8, 128), 1)
    sub = lax.broadcasted_iota(jnp.int32, (8, 128), 0)
    c16 = lane % 16
    group16 = lane // 16
    group4 = lane // 4

    count = [0]

    def remote(src, dst, who):
        i = count[0]
        count[0] += 1
        return pltpu.make_async_remote_copy(
            src_ref=src,
            dst_ref=dst,
            send_sem=ssem.at[i],
            recv_sem=rsem.at[i],
            device_id=who,
            device_id_type=MESH,
        )

    def row_copies(ref, lead, base, depth, up, down):
        out = []
        for z in range(4):
            row = base + 12 * z
            if up:
                out.append(
                    remote(
                        ref.at[lead + (pl.ds(row + 10 - depth, depth),)],
                        ref.at[lead + (pl.ds(row + 2 - depth, depth),)],
                        (xu, gy),
                    )
                )
            if down:
                out.append(
                    remote(
                        ref.at[lead + (pl.ds(row + 2, depth),)],
                        ref.at[lead + (pl.ds(row + 10, depth),)],
                        (xd, gy),
                    )
                )
        return out

    def pop_rows(ref, lead, base):
        return (
            row_copies(ref, lead + (pl.ds(0, 5),), base, 2, True, False)
            + row_copies(ref, lead + (pl.ds(14, 5),), base, 2, False, True)
            + row_copies(ref, lead + (pl.ds(5, 9),), base, 1, True, True)
        )

    def edge_copies(own, left, right, tiles):
        out = []
        for who, ref, src, dst in (
            ((xu, yr), left, (6, 2), 2),
            ((xd, yr), left, (0, 2), 12),
            ((xu, yl), right, (6, 2), 2),
            ((xd, yl), right, (0, 2), 12),
            ((gx, yr), left, (0, 8), 4),
            ((gx, yl), right, (0, 8), 4),
        ):
            out.append(
                remote(
                    own.at[tiles, pl.ds(*src)],
                    ref.at[tiles, pl.ds(dst, src[1])],
                    who,
                )
            )
        return out

    def pack(acc, v, z, slot):
        moved = pltpu.roll(v, (32 * z + 4 * slot + 2) % 128, 1)
        return moved if acc is None else jnp.where(group4 == 8 * z + slot, moved, acc)

    def strip_of(own, cy, left, right, slot):
        acc = None
        for z in range(4):
            for h in range(2):
                v = own(z, h)
                base = 32 * z + 16 * h
                w = jnp.where(
                    c16 < 8,
                    pltpu.roll(v, (base - 122 - cy) % 128, 1),
                    pltpu.roll(v, (base + 10 - cy) % 128, 1),
                )
                acc = w if acc is None else jnp.where(group16 == 2 * z + h, w, acc)
        odd = group16 % 2 == 1
        if cy >= 0 or True:
            r = [pltpu.roll(right(h), (16 * h + 4 - cy - 4 * slot) % 128, 1) for h in range(2)]
            r = jnp.where(odd, r[1], r[0])
            acc = jnp.where((c16 >= 6 - cy) & (c16 < 8), r, acc)
        l = [pltpu.roll(left(h), (16 * h + 8 - cy - 4 * slot) % 128, 1) for h in range(2)]
        l = jnp.where(odd, l[1], l[0])
        return jnp.where((c16 >= 8) & (c16 <= 9 - cy), l, acc)

    def store_strip(ref, f, v):
        ref[f, 1, 8:16, :] = v
        ref[f, 0, 8:16, :] = pltpu.roll(v, 32, 1)
        ref[f, 2, 8:16, :] = pltpu.roll(v, 96, 1)

    def strip_loader(ref):
        return lambda f, dx, dz: ref[f, 1 + dz, 8 + dx : 16 + dx, :]

    def flat_loader(ref, k):
        return lambda f, dx, dz: ref[f, pl.ds(8 * k + (16 + dx + 12 * dz), 8), :]

    def over_tiles(body):
        lax.fori_loop(0, 6, lambda k, carry: (body(k), carry)[1], 0)

    def saved(pops, dips, ref, tile0):
        acc = [None, None]
        for z in range(4):
            flow = [None] * 19
            dens = []
            for s in range(3):
                total = None
                for q in range(19):
                    f = pops[19 * s + q, z].astype(F32)
                    total = f if total is None else total + f
                    flow[q] = f if s == 0 else flow[q] + f
                dens.append(total)
            inverse = 1.0 / (dens[0] + dens[1] + dens[2])
            fields = list(dens)
            for i in range(3):
                amount = None
                for q in range(19):
                    c = VELOCITY[q][i]
                    if c != 0:
                        term = flow[q] if c > 0 else -flow[q]
                        amount = term if amount is None else amount + term
                fields.append(amount * inverse)
            fields.extend(dips[i, z].astype(F32) for i in range(3))
            for f in range(9):
                ref[f, 12 * z + 2 : 12 * z + 10, :] = fields[f]
                acc[f // 8] = pack(acc[f // 8], fields[f], z, f % 8)
        PO[tile0] = acc[0]
        PO[tile0 + 1] = acc[1]

    loads[0].wait()
    loads[1].wait()
    saved(NL, DL, FL, 9)

    loads[2].wait()

    def spread_pops(s, carry):
        acc = [None] * 3
        for o, q in enumerate(ORDER):
            for z in range(4):
                v = A[19 * s + q, (z + VELOCITY[q][2]) % 4]
                F[s, o, 8 + 12 * z + 2 : 8 + 12 * z + 10, :] = v
                acc[o // 8] = pack(acc[o // 8], v, z, o % 8)
        for i in range(3):
            PO[3 * s + i] = acc[i]
        return carry

    lax.fori_loop(0, 3, spread_pops, 0)

    pl.semaphore_wait(barrier, 8)
    every = (pl.ds(0, 9),)
    first = edge_copies(PO, PLX, PRX, pl.ds(0, 11))
    first += row_copies(FL, every, 0, 2, True, True)
    first += pop_rows(F, (pl.ds(0, 3),), 8)
    for copy in first:
        copy.start()

    loads[3].wait()
    loads[4].wait()
    saved(NE, DE, FE, 11)
    second_set = edge_copies(PO, PLX, PRX, pl.ds(11, 2)) + row_copies(FE, every, 0, 2, True, True)
    for copy in second_set:
        copy.start()

    def potentials(ref, strips):
        def body(k):
            rows = pl.ds(8 * k, 8)
            psi, fields = pick_potentials(
                [ref[s, rows, :] for s in range(3)], [ref[6 + i, rows, :] for i in range(3)]
            )
            for s in range(3):
                SI[s, k] = psi[s]
            for f in range(6):
                QM[f, pl.ds(16 + 8 * k, 8), :] = fields[f]
                QM[f, pl.ds(lax.rem(8 * k + 64, 96), 8), :] = fields[f]

        over_tiles(body)
        psi, fields = pick_potentials(
            [strips[s] for s in range(3)], [strips[6 + i] for i in range(3)]
        )
        for s in range(3):
            SI[s, 6] = psi[s]
        for f in range(6):
            store_strip(QS, f, fields[f])

    def all_thrusts(ref, strips):
        def body(k):
            rows = pl.ds(8 * k, 8)
            t = thrusts(flat_loader(QM, k), [ref[6 + i, rows, :] for i in range(3)])
            for f in range(9):
                TB[f, k] = t[f]

        over_tiles(body)
        t = thrusts(strip_loader(QS), [strips[6 + i] for i in range(3)])
        for f in range(9):
            TB[f, 6] = t[f]

    def field_strips(ref, strips, tile0):
        for f in range(9):
            tile, slot = tile0 + f // 8, f % 8
            strips[f] = strip_of(
                lambda z, h: ref[f, 12 * z + 4 * h : 12 * z + 4 * h + 8, :],
                0,
                lambda h: PLX[tile, 2 + 4 * h : 10 + 4 * h, :],
                lambda h: PRX[tile, 2 + 4 * h : 10 + 4 * h, :],
                slot,
            )

    def adjoint_stage(ref, strips, main_moments, strip_moments):
        def one(mom, k, rho, u, d, put_x, put_l):
            psi = [SI[s, k] for s in range(3)]
            t = [TB[f, k] for f in range(9)]
            fields, m, dens = local_adjoint(mom, rho, u, psi, t, d)
            for f in range(18):
                put_x(f, fields[f])
            for i in range(3):
                put_l(i, m[i])
                put_l(3 + i, dens[i])

        def body(k):
            rows = pl.ds(8 * k, 8)

            def put_x(f, v):
                XM[f, pl.ds(16 + 8 * k, 8), :] = v
                XM[f, pl.ds(lax.rem(8 * k + 64, 96), 8), :] = v

            def put_l(f, v):
                LM[f, rows, :] = v

            get = [ref[f, rows, :] for f in range(9)]
            one(main_moments(k), k, get[0:3], get[3:6], get[6:9], put_x, put_l)

        over_tiles(body)

        def put_x(f, v):
            store_strip(XS, f, v)

        def put_l(f, v):
            LS[f, 8:16, :] = v

        get = [strips[f] for f in range(9)]
        one(strip_moments(), 6, get[0:3], get[3:6], get[6:9], put_x, put_l)

    def spread_stage(ref, strips):
        def body(k):
            rows = pl.ds(8 * k, 8)
            new = spread(
                flat_loader(XM, k),
                [LM[3 + s, rows, :] for s in range(3)],
                [SI[s, k] for s in range(3)],
                [ref[6 + i, rows, :] for i in range(3)],
            )
            for s in range(3):
                LM[3 + s, rows, :] = new[s]

        over_tiles(body)
        new = spread(
            strip_loader(XS),
            [LS[3 + s, 8:16, :] for s in range(3)],
            [SI[s, 6] for s in range(3)],
            [strips[6 + i] for i in range(3)],
        )
        for s in range(3):
            LS[3 + s, 8:16, :] = new[s]

    def folded(ref, f):
        low = ref[f, 10:18, :]
        high = pltpu.roll(ref[f, 6:14, :], 112, 1)
        return jnp.where(sub < 4, low, high)

    def with_edges(v, edge, z):
        right = pltpu.roll(edge, (122 - 32 * z) % 128, 1)
        left = pltpu.roll(edge, (-32 * z - 10) % 128, 1)
        return jnp.where(lane >= 126, right, jnp.where(lane < 2, left, v))

    for copy in first:
        copy.wait_recv()

    acc = [None] * 3
    for o, q in enumerate(ORDER):
        cx, cy, cz = VELOCITY[q]
        tile, slot = 6 + o // 8, o % 8
        for z in range(4):
            v = shift_y(F[2, o, 8 + 12 * z + 2 + cx : 8 + 12 * z + 10 + cx, :], cy)
            if cy == -1:
                halo = pltpu.roll(
                    PLX[tile, 4 + cx : 12 + cx, :], (-(32 * z + 4 * slot + 1)) % 128, 1
                )
                v = jnp.where(lane == 0, halo, v)
            if cy == 1:
                halo = pltpu.roll(
                    PRX[tile, 4 + cx : 12 + cx, :], (127 - (32 * z + 4 * slot + 2)) % 128, 1
                )
                v = jnp.where(lane == 127, halo, v)
            to = (z - cz) % 4
            FG[o, 8 + 12 * to + 2 : 8 + 12 * to + 10, :] = v
            acc[o // 8] = pack(acc[o // 8], v, to, slot)
    for i in range(3):
        PGO[i] = acc[i]
    kept = edge_copies(PGO, PGL, PGR, pl.ds(0, 3)) + pop_rows(FG, (), 8)
    for copy in kept:
        copy.start()

    field_strips(FL, SL, 9)
    potentials(FL, SL)
    all_thrusts(FL, SL)

    def pop_strips(s, carry):
        for o, q in enumerate(ORDER):
            cx, cy, _ = VELOCITY[q]
            SA[19 * s + o] = strip_of(
                lambda z, h: F[
                    s, o, 8 + 12 * z + 4 * h + cx : 8 + 12 * z + 4 * h + cx + 8, :
                ],
                cy,
                lambda h: PLX[3 * s + o // 8, 2 + 4 * h + cx : 10 + 4 * h + cx, :],
                lambda h: PRX[3 * s + o // 8, 2 + 4 * h + cx : 10 + 4 * h + cx, :],
                o % 8,
            )
        return carry

    lax.fori_loop(0, 3, pop_strips, 0)

    def pulled_moments(k):
        out = []
        for s in range(3):
            g = {}
            for o, q in enumerate(ORDER):
                cx, cy, _ = VELOCITY[q]
                g[q] = shift_y(F[s, o, pl.ds(8 * k + (8 + cx), 8), :], cy)
            out.append(moments_of(g))
        return out

    def pulled_strip_moments():
        return [moments_of({q: SA[19 * s + SLOT[q]] for q in range(19)}) for s in range(3)]

    adjoint_stage(FL, SL, pulled_moments, pulled_strip_moments)
    spread_stage(FL, SL)

    acc = None
    for f in range(6):
        edge = folded(LS, f)
        for z in range(4):
            v = with_edges(LM[f, 12 * z + 2 : 12 * z + 10, :], edge, z)
            FM[f, 16 + 12 * z + 2 : 16 + 12 * z + 10, :] = v
            acc = pack(acc, v, z, f)
    PMO[0] = acc
    middle = edge_copies(PMO, PML, PMR, pl.ds(0, 1)) + row_copies(
        FM, (pl.ds(0, 6),), 16, 2, True, True
    )
    for copy in middle:
        copy.start()

    for copy in second_set:
        copy.wait_recv()
    field_strips(FE, SE, 11)
    potentials(FE, SE)
    all_thrusts(FE, SE)

    for copy in kept:
        copy.wait_recv()
    for o, q in enumerate(ORDER):
        cx, cy, _ = VELOCITY[q]
        SG[o] = strip_of(
            lambda z, h: FG[o, 8 + 12 * z + 4 * h + cx : 8 + 12 * z + 4 * h + cx + 8, :],
            cy,
            lambda h: PGL[o // 8, 2 + 4 * h + cx : 10 + 4 * h + cx, :],
            lambda h: PGR[o // 8, 2 + 4 * h + cx : 10 + 4 * h + cx, :],
            o % 8,
        )

    for copy in middle:
        copy.wait_recv()
    for f in range(6):
        FM[f, 0:16, :] = FM[f, 48:64, :]
        FM[f, 64:80, :] = FM[f, 16:32, :]
        store_strip(
            MS,
            f,
            strip_of(
                lambda z, h: FM[f, 16 + 12 * z + 4 * h : 16 + 12 * z + 4 * h + 8, :],
                0,
                lambda h: PML[0, 2 + 4 * h : 10 + 4 * h, :],
                lambda h: PMR[0, 2 + 4 * h : 10 + 4 * h, :],
                f,
            ),
        )

    def middle_moments(k):
        g = {}
        for o, q in enumerate(ORDER):
            cx, cy, _ = VELOCITY[q]
            g[q] = shift_y(FG[o, pl.ds(8 * k + (8 + cx), 8), :], cy)
        return late_moments(flat_loader(FM, k), g)

    def middle_strip_moments():
        return late_moments(strip_loader(MS), {q: SG[SLOT[q]] for q in range(19)})

    adjoint_stage(FE, SE, middle_moments, middle_strip_moments)
    spread_stage(FE, SE)

    def along(q, m):
        out = None
        for i in range(3):
            c = VELOCITY[q][i]
            if c != 0:
                term = m[i] if c > 0 else -m[i]
                out = term if out is None else out + term
        return out

    def plus(base, term):
        return base if term is None else base + term

    strip = strip_loader(MS)
    for o, q in enumerate(ORDER):
        cx, cy, cz = VELOCITY[q]
        if cy != 0:
            v = plus(strip(5, cx, cz), along(q, [strip(i, cx, cz) for i in range(3)]))
            TS[o, 8:16, :] = shift_y(v, cy) + 0.2 * SG[o]

    edges = [folded(LS, f) for f in range(6)]
    for z in range(4):
        fin = [with_edges(LM[f, 12 * z + 2 : 12 * z + 10, :], edges[f], z) for f in range(6)]
        for q in range(19):
            cx, cy, cz = VELOCITY[q]
            term = along(q, fin[0:3])
            OUT[q, z] = plus(fin[3], term)
            OUT[19 + q, z] = plus(fin[4], term)
            o = SLOT[q]
            row = 12 * z + 2 + cx
            mid = [FM[i, 16 + row + 12 * cz : 24 + row + 12 * cz, :] for i in (0, 1, 2, 5)]
            v = plus(mid[3], along(q, mid[0:3])) + 0.2 * FG[o, 8 + row : 16 + row, :]
            v = shift_y(v, cy)
            if cy != 0:
                v = with_edges(v, folded(TS, o), z)
            OUT[38 + q, z] = plus(fin[5], term) + 0.2 * v

    done = pltpu.make_async_copy(OUT, o_out, lsem.at[5])
    done.start()
    for copy in first + second_set + kept + middle:
        copy.wait_send()
    done.wait()


N_REMOTE = 6 + 8 + 16 + 6 + 8 + 6 + 16 + 6 + 8


def block(size_x, size_y, *args):
    def vmem(*shape, dtype=F32):
        return pltpu.VMEM(shape, dtype)

    bf = jnp.bfloat16
    scratch = [
        vmem(57, 4, 8, 128),
        vmem(57, 4, 8, 128, dtype=bf),
        vmem(57, 4, 8, 128, dtype=bf),
        vmem(3, 4, 8, 128, dtype=bf),
        vmem(3, 4, 8, 128, dtype=bf),
        vmem(57, 4, 8, 128),
        vmem(3, 19, 64, 128),
        vmem(9, 48, 128),
        vmem(9, 48, 128),
        vmem(6, 80, 128),
        vmem(19, 64, 128),
        vmem(13, 8, 128),
        vmem(13, 16, 128),
        vmem(13, 16, 128),
        vmem(3, 8, 128),
        vmem(3, 16, 128),
        vmem(3, 16, 128),
        vmem(1, 8, 128),
        vmem(1, 16, 128),
        vmem(1, 16, 128),
        vmem(57, 8, 128),
        vmem(19, 8, 128),
        vmem(9, 8, 128),
        vmem(9, 8, 128),
        vmem(6, 96, 128),
        vmem(6, 3, 24, 128),
        vmem(9, 7, 8, 128),
        vmem(3, 7, 8, 128),
        vmem(18, 96, 128),
        vmem(18, 3, 24, 128),
        vmem(6, 48, 128),
        vmem(6, 24, 128),
        vmem(6, 3, 24, 128),
        vmem(19, 24, 128),
        pltpu.SemaphoreType.DMA((6,)),
        pltpu.SemaphoreType.DMA((N_REMOTE,)),
        pltpu.SemaphoreType.DMA((N_REMOTE,)),
    ]
    return pl.pallas_call(
        lambda *refs: kernel(size_x, size_y, *refs),
        out_shape=jax.ShapeDtypeStruct((57, 4, 8, 128), F32),
        in_specs=[pl.BlockSpec(memory_space=pl.ANY)] * 5,
        out_specs=pl.BlockSpec(memory_space=pl.ANY),
        scratch_shapes=scratch,
        compiler_params=pltpu.CompilerParams(collective_id=0, has_side_effects=True),
        name="lattice_adjoint",
    )(*args)


def solution(mesh):
    size_x, size_y = mesh.shape["gx"], mesh.shape["gy"]
    spec = P(None, None, "gx", "gy")
    return jax.shard_map(
        lambda *args: block(size_x, size_y, *args),
        mesh=mesh,
        in_specs=(spec,) * 5,
        out_specs=spec,
        check_vma=False,
    )
```

profile of v0, /device:TPU:1, one launch (start us, length us, event | category | flops | bytes accessed | tf_op | source)
XLA Modules:
  0.0 32.9 jit_solution(18331988226565921032)
XLA Ops:
  0.0 30.7 %lattice_adjoint.1 = f32[57,4,8,128]{3,2,1,0:T(8,128)} custom-call(f32[57,4,8,128]{3,2,1,0:T(8,128)} %refs_0_.1, bf16[57,4,8,128]{3,2,1,0:T(8,128)(2,1)} %refs_1_.1, bf16[57,4,8,128]{3,2,1,0:T(8,128)(2,1)} %refs_2_.1, bf16[3,4,8,128]{3,2,1,0:T(8,128)(2,1)} %refs_3_.1, bf16[3,4,8,128]{3,2,1,0:T(8,128)(2,1)} %refs_4_.1), custom_call_target="tpu_custom_call" | custom-call | tf_op jit(solution)/shard_map/lattice_adjoint/pallas_call | solution.py:849
  30.7 2.2 %copy.7 = f32[57,4,8,128]{3,2,1,0:T(8,128)} copy(f32[57,4,8,128]{3,2,1,0:T(8,128)} %lattice_adjoint.1) | data formatting | bytes 1867776
where the time goes:
time: 33 us; the launch traced here: 32.9 us
  Pallas kernels  30.7 us (93%)
  local copies, waits for them, and re-layouts  2.17 us (7%)
    pallas_call x1, Pallas kernels, block(): pl.pallas_call(lambda *refs: kernel(size_x, size_y, *refs), out_shape=jax...  30.7 us
    unnamed x1, local copies, waits for them, and re-layouts  2.17 us

commit v1 on v0

--- a/solution.py
+++ b/solution.py
@@ -286,6 +286,19 @@
     return out
 
 
+def along(q, m):
+    out = None
+    for i in range(3):
+        c = VELOCITY[q][i]
+        if c != 0:
+            term = m[i] if c > 0 else -m[i]
+            out = term if out is None else out + term
+    return out
+
+def plus(base, term):
+    return base if term is None else base + term
+
+
 def kernel(
     size_x,
     size_y,
@@ -294,13 +307,12 @@
     pl_in,
     de_in,
     dl_in,
-    o_out,
+    FIN,
     A,
     NE,
     NL,
     DE,
     DL,
-    OUT,
     F,
     FL,
     FE,
@@ -454,7 +466,7 @@
         return lambda f, dx, dz: ref[f, pl.ds(8 * k + (16 + dx + 12 * dz), 8), :]
 
     def over_tiles(body):
-        lax.fori_loop(0, 6, lambda k, carry: (body(k), carry)[1], 0)
+        lax.fori_loop(0, 6, lambda k, carry: (body(k), carry)[1], 0, unroll=3)
 
     def saved(pops, dips, ref, tile0):
         acc = [None, None]
@@ -508,8 +520,8 @@
     every = (pl.ds(0, 9),)
     first = edge_copies(PO, PLX, PRX, pl.ds(0, 11))
     first += row_copies(FL, every, 0, 2, True, True)
-    first += pop_rows(F, (pl.ds(0, 3),), 8)
-    for copy in first:
+    rows = pop_rows(F, (pl.ds(0, 3),), 8)
+    for copy in first + rows:
         copy.start()
 
     loads[3].wait()
@@ -631,6 +643,11 @@
         return jnp.where(lane >= 126, right, jnp.where(lane < 2, left, v))
 
     for copy in first:
+        copy.wait_recv()
+    field_strips(FL, SL, 9)
+    potentials(FL, SL)
+    all_thrusts(FL, SL)
+    for copy in rows:
         copy.wait_recv()
 
     acc = [None] * 3
@@ -658,10 +675,6 @@
     for copy in kept:
         copy.start()
 
-    field_strips(FL, SL, 9)
-    potentials(FL, SL)
-    all_thrusts(FL, SL)
-
     def pop_strips(s, carry):
         for o, q in enumerate(ORDER):
             cx, cy, _ = VELOCITY[q]
@@ -756,18 +769,6 @@
     adjoint_stage(FE, SE, middle_moments, middle_strip_moments)
     spread_stage(FE, SE)
 
-    def along(q, m):
-        out = None
-        for i in range(3):
-            c = VELOCITY[q][i]
-            if c != 0:
-                term = m[i] if c > 0 else -m[i]
-                out = term if out is None else out + term
-        return out
-
-    def plus(base, term):
-        return base if term is None else base + term
-
     strip = strip_loader(MS)
     for o, q in enumerate(ORDER):
         cx, cy, cz = VELOCITY[q]
@@ -777,26 +778,36 @@
 
     edges = [folded(LS, f) for f in range(6)]
     for z in range(4):
-        fin = [with_edges(LM[f, 12 * z + 2 : 12 * z + 10, :], edges[f], z) for f in range(6)]
-        for q in range(19):
+        for f in range(6):
+            FIN[f, z] = with_edges(LM[f, 12 * z + 2 : 12 * z + 10, :], edges[f], z)
+        for o, q in enumerate(ORDER):
             cx, cy, cz = VELOCITY[q]
-            term = along(q, fin[0:3])
-            OUT[q, z] = plus(fin[3], term)
-            OUT[19 + q, z] = plus(fin[4], term)
-            o = SLOT[q]
             row = 12 * z + 2 + cx
             mid = [FM[i, 16 + row + 12 * cz : 24 + row + 12 * cz, :] for i in (0, 1, 2, 5)]
             v = plus(mid[3], along(q, mid[0:3])) + 0.2 * FG[o, 8 + row : 16 + row, :]
             v = shift_y(v, cy)
             if cy != 0:
                 v = with_edges(v, folded(TS, o), z)
-            OUT[38 + q, z] = plus(fin[5], term) + 0.2 * v
-
-    done = pltpu.make_async_copy(OUT, o_out, lsem.at[5])
-    done.start()
-    for copy in first + second_set + kept + middle:
+            FIN[6 + q, z] = 0.2 * v
+
+    for copy in first + rows + second_set + kept + middle:
         copy.wait_send()
-    done.wait()
+
+
+def expand(fin, out, OUT, sem):
+    copies = []
+    for s in range(3):
+        for z in range(4):
+            m = [fin[i, z] for i in range(3)]
+            base = fin[3 + s, z]
+            for q in range(19):
+                v = plus(base, along(q, m))
+                OUT[19 * s + q, z] = v + fin[6 + q, z] if s == 2 else v
+        part = pl.ds(19 * s, 19)
+        copies.append(pltpu.make_async_copy(OUT.at[part], out.at[part], sem.at[s]))
+        copies[s].start()
+    for copy in copies:
+        copy.wait()
 
 
 N_REMOTE = 6 + 8 + 16 + 6 + 8 + 6 + 16 + 6 + 8
@@ -813,7 +824,6 @@
         vmem(57, 4, 8, 128, dtype=bf),
         vmem(3, 4, 8, 128, dtype=bf),
         vmem(3, 4, 8, 128, dtype=bf),
-        vmem(57, 4, 8, 128),
         vmem(3, 19, 64, 128),
         vmem(9, 48, 128),
         vmem(9, 48, 128),
@@ -842,19 +852,30 @@
         vmem(6, 24, 128),
         vmem(6, 3, 24, 128),
         vmem(19, 24, 128),
-        pltpu.SemaphoreType.DMA((6,)),
+        pltpu.SemaphoreType.DMA((5,)),
         pltpu.SemaphoreType.DMA((N_REMOTE,)),
         pltpu.SemaphoreType.DMA((N_REMOTE,)),
     ]
+    fin = pl.pallas_call(
+        lambda *refs: kernel(size_x, size_y, *refs),
+        out_shape=jax.ShapeDtypeStruct((25, 4, 8, 128), F32),
+        in_specs=[pl.BlockSpec(memory_space=pltpu.HBM)] * 5,
+        out_specs=pl.BlockSpec(memory_space=pltpu.VMEM),
+        scratch_shapes=scratch,
+        compiler_params=pltpu.CompilerParams(
+            collective_id=0, has_side_effects=True, vmem_limit_bytes=24 << 20
+        ),
+        name="lattice_adjoint",
+    )(*[pltpu.with_memory_space_constraint(a, pltpu.HBM) for a in args])
     return pl.pallas_call(
-        lambda *refs: kernel(size_x, size_y, *refs),
+        expand,
         out_shape=jax.ShapeDtypeStruct((57, 4, 8, 128), F32),
-        in_specs=[pl.BlockSpec(memory_space=pl.ANY)] * 5,
-        out_specs=pl.BlockSpec(memory_space=pl.ANY),
-        scratch_shapes=scratch,
-        compiler_params=pltpu.CompilerParams(collective_id=0, has_side_effects=True),
-        name="lattice_adjoint",
-    )(*args)
+        in_specs=[pl.BlockSpec(memory_space=pltpu.VMEM)],
+        out_specs=pl.BlockSpec(memory_space=pltpu.HBM),
+        scratch_shapes=[vmem(57, 4, 8, 128), pltpu.SemaphoreType.DMA((3,))],
+        compiler_params=pltpu.CompilerParams(vmem_limit_bytes=8 << 20),
+        name="lattice_expand",
+    )(fin)
 
 
 def solution(mesh):

time: 33 us -> 28.4 us (0.86)
  Pallas kernels: 30.7 us -> 28.3 us
  local copies, waits for them, and re-layouts: 2.17 us -> 0 us
    pallas_call x1, Pallas kernels: 30.7 us -> 27.3 us  [block(): pl.pallas_call(lambda *refs: kernel(size_x, size_y, *refs), out_shape=jax...]
    unnamed x1 -> x0, local copies, waits for them, and re-layouts: 2.17 us -> none
    pallas_call x0 -> x1, Pallas kernels: none -> 0.99 us  [block(): pl.pallas_call(expand, out_shape=jax.ShapeDtypeStruct((57, 4, 8, 128), F3...]
where the time goes in v1:
time: 28.4 us; the launch traced here: 28.3 us
  Pallas kernels  28.3 us (100%)
    pallas_call x1, Pallas kernels, block(): pl.pallas_call(lambda *refs: kernel(size_x, size_y, *refs), out_shape=jax...  27.3 us
    pallas_call x1, Pallas kernels, block(): pl.pallas_call(expand, out_shape=jax.ShapeDtypeStruct((57, 4, 8, 128), F3...  0.99 us

profile of v1, /device:TPU:1, one launch (start us, length us, event | category | flops | bytes accessed | tf_op | source)
XLA Modules:
  0.0 28.3 jit_solution(17498380910104752294)
XLA Ops:
  0.0 27.3 %lattice_adjoint.1.fin = f32[25,4,8,128]{3,2,1,0:T(8,128)S(1)} custom-call(f32[57,4,8,128]{3,2,1,0:T(8,128)} %refs_0_.1, bf16[57,4,8,128]{3,2,1,0:T(8,128)(2,1)} %refs_1_.1, bf16[57,4,8,128]{3,2,1,0:T(8,128)(2,1)} %refs_2_.1, bf16[3,4,8,128]{3,2,1,0:T(8,128)(2,1)} %refs_3_.1, bf16[3,4,8,128]{3,2,1,0:T(8,128)(2,1)} %refs_4_.1), custom_call_target="tpu_custom_call" | custom-call | tf_op jit(solution)/shard_map/lattice_adjoint/pallas_call | solution.py:859
  27.3 1.0 %lattice_expand.1 = f32[57,4,8,128]{3,2,1,0:T(8,128)} custom-call(f32[25,4,8,128]{3,2,1,0:T(8,128)S(1)} %lattice_adjoint.1.fin), custom_call_target="tpu_custom_call" | custom-call | tf_op jit(solution)/shard_map/lattice_expand/pallas_call | solution.py:870

commit v2 on v1

--- a/solution.py
+++ b/solution.py
@@ -1,3 +1,5 @@
+import math
+
 import jax
 import jax.numpy as jnp
 from jax import lax
@@ -32,6 +34,7 @@
 ORDER = (1, 5, 7, 9, 11, 2, 3, 12, 13, 14, 15, 16, 17, 18, 0, 4, 6, 8, 10)
 SLOT = {q: i for i, q in enumerate(ORDER)}
 F32 = jnp.float32
+N_SETS = 5
 
 
 def up_y(v):
@@ -341,6 +344,7 @@
     LS,
     MS,
     TS,
+    W,
     lsem,
     ssem,
     rsem,
@@ -367,19 +371,32 @@
     group16 = lane // 16
     group4 = lane // 4
 
-    count = [0]
+    current = [0]
+    sent = [0] * N_SETS
 
     def remote(src, dst, who):
-        i = count[0]
-        count[0] += 1
+        sent[current[0]] += math.prod(src.shape) // 128
         return pltpu.make_async_remote_copy(
             src_ref=src,
             dst_ref=dst,
-            send_sem=ssem.at[i],
-            recv_sem=rsem.at[i],
+            send_sem=ssem.at[0],
+            recv_sem=rsem.at[current[0]],
             device_id=who,
             device_id_type=MESH,
         )
+
+    def begin(copies):
+        for copy in copies:
+            copy.start()
+        current[0] += 1
+        return current[0] - 1
+
+    def wait_rows(rows, sem):
+        span = W.at[pl.ds(0, rows)]
+        pltpu.make_async_copy(span, span, sem).wait()
+
+    def arrive(number):
+        wait_rows(sent[number], rsem.at[number])
 
     def row_copies(ref, lead, base, depth, up, down):
         out = []
@@ -520,16 +537,15 @@
     every = (pl.ds(0, 9),)
     first = edge_copies(PO, PLX, PRX, pl.ds(0, 11))
     first += row_copies(FL, every, 0, 2, True, True)
-    rows = pop_rows(F, (pl.ds(0, 3),), 8)
-    for copy in first + rows:
-        copy.start()
+    first = begin(first)
+    rows = begin(pop_rows(F, (pl.ds(0, 3),), 8))
 
     loads[3].wait()
     loads[4].wait()
     saved(NE, DE, FE, 11)
-    second_set = edge_copies(PO, PLX, PRX, pl.ds(11, 2)) + row_copies(FE, every, 0, 2, True, True)
-    for copy in second_set:
-        copy.start()
+    second_set = begin(
+        edge_copies(PO, PLX, PRX, pl.ds(11, 2)) + row_copies(FE, every, 0, 2, True, True)
+    )
 
     def potentials(ref, strips):
         def body(k):
@@ -642,13 +658,11 @@
         left = pltpu.roll(edge, (-32 * z - 10) % 128, 1)
         return jnp.where(lane >= 126, right, jnp.where(lane < 2, left, v))
 
-    for copy in first:
-        copy.wait_recv()
+    arrive(first)
     field_strips(FL, SL, 9)
     potentials(FL, SL)
     all_thrusts(FL, SL)
-    for copy in rows:
-        copy.wait_recv()
+    arrive(rows)
 
     acc = [None] * 3
     for o, q in enumerate(ORDER):
@@ -671,9 +685,11 @@
             acc[o // 8] = pack(acc[o // 8], v, to, slot)
     for i in range(3):
         PGO[i] = acc[i]
-    kept = edge_copies(PGO, PGL, PGR, pl.ds(0, 3)) + pop_rows(FG, (), 8)
-    for copy in kept:
-        copy.start()
+    kept = begin(
+        edge_copies(PGO, PGL, PGR, pl.ds(0, 3))
+        + row_copies(FG, (pl.ds(0, 14),), 8, 2, True, False)
+        + row_copies(FG, (pl.ds(5, 14),), 8, 2, False, True)
+    )
 
     def pop_strips(s, carry):
         for o, q in enumerate(ORDER):
@@ -715,20 +731,17 @@
             FM[f, 16 + 12 * z + 2 : 16 + 12 * z + 10, :] = v
             acc = pack(acc, v, z, f)
     PMO[0] = acc
-    middle = edge_copies(PMO, PML, PMR, pl.ds(0, 1)) + row_copies(
-        FM, (pl.ds(0, 6),), 16, 2, True, True
-    )
-    for copy in middle:
-        copy.start()
-
-    for copy in second_set:
-        copy.wait_recv()
+    middle = begin(
+        edge_copies(PMO, PML, PMR, pl.ds(0, 1))
+        + row_copies(FM, (pl.ds(0, 6),), 16, 2, True, True)
+    )
+
+    arrive(second_set)
     field_strips(FE, SE, 11)
     potentials(FE, SE)
     all_thrusts(FE, SE)
 
-    for copy in kept:
-        copy.wait_recv()
+    arrive(kept)
     for o, q in enumerate(ORDER):
         cx, cy, _ = VELOCITY[q]
         SG[o] = strip_of(
@@ -739,8 +752,7 @@
             o % 8,
         )
 
-    for copy in middle:
-        copy.wait_recv()
+    arrive(middle)
     for f in range(6):
         FM[f, 0:16, :] = FM[f, 48:64, :]
         FM[f, 64:80, :] = FM[f, 16:32, :]
@@ -790,8 +802,7 @@
                 v = with_edges(v, folded(TS, o), z)
             FIN[6 + q, z] = 0.2 * v
 
-    for copy in first + rows + second_set + kept + middle:
-        copy.wait_send()
+    wait_rows(sum(sent), ssem.at[0])
 
 
 def expand(fin, out, OUT, sem):
@@ -808,9 +819,6 @@
         copies[s].start()
     for copy in copies:
         copy.wait()
-
-
-N_REMOTE = 6 + 8 + 16 + 6 + 8 + 6 + 16 + 6 + 8
 
 
 def block(size_x, size_y, *args):
@@ -852,9 +860,10 @@
         vmem(6, 24, 128),
         vmem(6, 3, 24, 128),
         vmem(19, 24, 128),
+        vmem(3072, 128),
         pltpu.SemaphoreType.DMA((5,)),
-        pltpu.SemaphoreType.DMA((N_REMOTE,)),
-        pltpu.SemaphoreType.DMA((N_REMOTE,)),
+        pltpu.SemaphoreType.DMA((1,)),
+        pltpu.SemaphoreType.DMA((N_SETS,)),
     ]
     fin = pl.pallas_call(
         lambda *refs: kernel(size_x, size_y, *refs),

time: 28.4 us -> 26.8 us (0.944)
  Pallas kernels: 28.3 us -> 26.7 us
    pallas_call x1, Pallas kernels: 27.3 us -> 25.7 us  [block(): pl.pallas_call(lambda *refs: kernel(size_x, size_y, *refs), out_shape=jax...]
where the time goes in v2:
time: 26.8 us; the launch traced here: 26.7 us
  Pallas kernels  26.7 us (100%)
    pallas_call x1, Pallas kernels, block(): pl.pallas_call(lambda *refs: kernel(size_x, size_y, *refs), out_shape=jax...  25.7 us
    pallas_call x1, Pallas kernels, block(): pl.pallas_call(expand, out_shape=jax.ShapeDtypeStruct((57, 4, 8, 128), F3...  0.99 us

profile of v2, /device:TPU:1, one launch (start us, length us, event | category | flops | bytes accessed | tf_op | source)
XLA Modules:
  0.0 26.7 jit_solution(14795449708970736601)
XLA Ops:
  0.0 25.7 %lattice_adjoint.1.fin = f32[25,4,8,128]{3,2,1,0:T(8,128)S(1)} custom-call(f32[57,4,8,128]{3,2,1,0:T(8,128)} %refs_0_.1, bf16[57,4,8,128]{3,2,1,0:T(8,128)(2,1)} %refs_1_.1, bf16[57,4,8,128]{3,2,1,0:T(8,128)(2,1)} %refs_2_.1, bf16[3,4,8,128]{3,2,1,0:T(8,128)(2,1)} %refs_3_.1, bf16[3,4,8,128]{3,2,1,0:T(8,128)(2,1)} %refs_4_.1), custom_call_target="tpu_custom_call" | custom-call | tf_op jit(solution)/shard_map/lattice_adjoint/pallas_call | solution.py:868
  25.7 1.0 %lattice_expand.1 = f32[57,4,8,128]{3,2,1,0:T(8,128)} custom-call(f32[25,4,8,128]{3,2,1,0:T(8,128)S(1)} %lattice_adjoint.1.fin), custom_call_target="tpu_custom_call" | custom-call | tf_op jit(solution)/shard_map/lattice_expand/pallas_call | solution.py:879

commit v3 on v2

--- a/solution.py
+++ b/solution.py
@@ -33,8 +33,10 @@
 G = ((0.0, 1.2, -0.6), (1.2, 0.0, -0.6), (-0.6, -0.6, -0.3))
 ORDER = (1, 5, 7, 9, 11, 2, 3, 12, 13, 14, 15, 16, 17, 18, 0, 4, 6, 8, 10)
 SLOT = {q: i for i, q in enumerate(ORDER)}
+RIGHTWARD = tuple(o for o, q in enumerate(ORDER) if VELOCITY[q][1] <= 0)
+LEFTWARD = tuple(o for o, q in enumerate(ORDER) if VELOCITY[q][1] >= 0)
 F32 = jnp.float32
-N_SETS = 5
+N_SETS = 6
 
 
 def up_y(v):
@@ -190,14 +192,13 @@
     return t0 + t1 + t2
 
 
-def local_adjoint(mom, rho, u, psi, t, d):
-    x, e_val, wt, ratio = [], [], [], []
+def local_adjoint(mom, rho, u, psi, t, velocity, ratio, inverse):
+    x, e_val, wt = [], [], []
     m = [None] * 3
     for s in range(3):
         a, b, c = mom[s]
-        ratio.append(TAU[s] * psi[s] / rho[s])
         ts = t[3 * s : 3 * s + 3]
-        v = [u[i] + ratio[s] * ts[i] for i in range(3)]
+        v = velocity[3 * s : 3 * s + 3]
         cv = (
             c["xx"] * v[0] + c["xy"] * v[1] + c["xz"] * v[2],
             c["xy"] * v[0] + c["yy"] * v[1] + c["yz"] * v[2],
@@ -216,13 +217,15 @@
             m[i] = term if s == 0 else m[i] + term
         tp = TAU[s] * psi[s]
         x.extend(tp * w[i] for i in range(3))
-    inverse = 1.0 / (rho[0] + rho[1] + rho[2])
     m = [m[i] * inverse for i in range(3)]
     mu = m[0] * u[0] + m[1] * u[1] + m[2] * u[2]
     dens = [e_val[s] + wt[s] * (TAU[s] * (1.0 - psi[s]) - ratio[s]) - mu for s in range(3)]
-    y = x[6:9]
+    return x, m, dens
+
+
+def products(y, d):
     kxx, kyy, kzz = y[0] * d[0], y[1] * d[1], y[2] * d[2]
-    kept = [
+    return [
         kxx,
         kyy,
         kzz,
@@ -233,7 +236,6 @@
         kyy + kzz,
         kxx + kzz,
     ]
-    return x + kept, m, dens
 
 
 def spread(ld, dens, psi, d):
@@ -255,7 +257,10 @@
     return [dens[s] + (k * (1.0 - psi[s])) * back[s] for s in range(3)]
 
 
-def late_moments(ld, pulled):
+KEYS = ("xx", "yy", "zz", "xy", "xz", "yz")
+
+
+def late_moments(ld, extra):
     x, y, z = (near(ld, i) for i in range(3))
     axx, azz = 2.0 * x["dx"], 2.0 * z["dz"]
     ayy = 2.0 * (up_y(y["c"]) - dn_y(y["c"]))
@@ -272,7 +277,6 @@
         yz=up_y(y["dz"] + z["sz"]) + dn_y(y["dz"] - z["sz"]),
         xz=corner_z(x) + corner_x(z),
     )
-    extra = moments_of(pulled)
     out = []
     for s in range(3):
         n = near(ld, 3 + s)
@@ -282,9 +286,9 @@
         b = [g[i] + b_m[i] for i in range(3)]
         c = {key: c[key] + c_m[key] for key in c}
         if s == 2:
-            a = a + 0.2 * extra[0]
-            b = [b[i] + 0.2 * extra[1][i] for i in range(3)]
-            c = {key: c[key] + 0.2 * extra[2][key] for key in c}
+            a = a + extra[0]
+            b = [b[i] + extra[1 + i] for i in range(3)]
+            c = {key: c[key] + extra[4 + i] for i, key in enumerate(KEYS)}
         out.append((a, b, c))
     return out
 
@@ -324,19 +328,25 @@
     PO,
     PLX,
     PRX,
+    PAO,
+    PER,
+    PEL,
+    PAL,
+    PAR,
     PGO,
     PGL,
     PGR,
     PMO,
     PML,
     PMR,
-    SA,
+    SX,
     SG,
     SL,
     SE,
     QM,
     QS,
     TB,
+    EX,
     SI,
     XM,
     XS,
@@ -385,11 +395,14 @@
             device_id_type=MESH,
         )
 
+    def close():
+        current[0] += 1
+        return current[0] - 1
+
     def begin(copies):
         for copy in copies:
             copy.start()
-        current[0] += 1
-        return current[0] - 1
+        return close()
 
     def wait_rows(rows, sem):
         span = W.at[pl.ds(0, rows)]
@@ -427,7 +440,8 @@
             + row_copies(ref, lead + (pl.ds(5, 9),), base, 1, True, True)
         )
 
-    def edge_copies(own, left, right, tiles):
+    def edge_copies(own, left, right, tiles, other=None):
+        other = own if other is None else other
         out = []
         for who, ref, src, dst in (
             ((xu, yr), left, (6, 2), 2),
@@ -439,7 +453,7 @@
         ):
             out.append(
                 remote(
-                    own.at[tiles, pl.ds(*src)],
+                    (own if ref is left else other).at[tiles, pl.ds(*src)],
                     ref.at[tiles, pl.ds(dst, src[1])],
                     who,
                 )
@@ -450,7 +464,9 @@
         moved = pltpu.roll(v, (32 * z + 4 * slot + 2) % 128, 1)
         return moved if acc is None else jnp.where(group4 == 8 * z + slot, moved, acc)
 
-    def strip_of(own, cy, left, right, slot):
+    odd = group16 % 2 == 1
+
+    def own_strip(own, cy):
         acc = None
         for z in range(4):
             for h in range(2):
@@ -462,11 +478,12 @@
                     pltpu.roll(v, (base + 10 - cy) % 128, 1),
                 )
                 acc = w if acc is None else jnp.where(group16 == 2 * z + h, w, acc)
-        odd = group16 % 2 == 1
-        if cy >= 0 or True:
-            r = [pltpu.roll(right(h), (16 * h + 4 - cy - 4 * slot) % 128, 1) for h in range(2)]
-            r = jnp.where(odd, r[1], r[0])
-            acc = jnp.where((c16 >= 6 - cy) & (c16 < 8), r, acc)
+        return acc
+
+    def strip_of(own, cy, left, right, slot):
+        acc = own_strip(own, cy)
+        r = [pltpu.roll(right(h), (16 * h + 4 - cy - 4 * slot) % 128, 1) for h in range(2)]
+        acc = jnp.where((c16 >= 6 - cy) & (c16 < 8), jnp.where(odd, r[1], r[0]), acc)
         l = [pltpu.roll(left(h), (16 * h + 8 - cy - 4 * slot) % 128, 1) for h in range(2)]
         l = jnp.where(odd, l[1], l[0])
         return jnp.where((c16 >= 8) & (c16 <= 9 - cy), l, acc)
@@ -516,35 +533,51 @@
 
     loads[0].wait()
     loads[1].wait()
-    saved(NL, DL, FL, 9)
+    saved(NL, DL, FL, 0)
 
     loads[2].wait()
 
-    def spread_pops(s, carry):
-        acc = [None] * 3
-        for o, q in enumerate(ORDER):
+    pair = (lane % 8) // 2
+    narrow = [[None] * 4, [None] * 4]
+    for o, q in enumerate(ORDER):
+        acc = None
+        for s in range(3):
             for z in range(4):
                 v = A[19 * s + q, (z + VELOCITY[q][2]) % 4]
                 F[s, o, 8 + 12 * z + 2 : 8 + 12 * z + 10, :] = v
-                acc[o // 8] = pack(acc[o // 8], v, z, o % 8)
-        for i in range(3):
-            PO[3 * s + i] = acc[i]
-        return carry
-
-    lax.fori_loop(0, 3, spread_pops, 0)
+                acc = pack(acc, v, z, 2 * s)
+        PAO[o, 4:12, :] = jnp.where(group4 % 2 == 1, pltpu.roll(acc, 4, 1), acc)
+        for side, group in enumerate((RIGHTWARD, LEFTWARD)):
+            if o in group:
+                i, j = divmod(group.index(o), 4)
+                moved = pltpu.roll(acc, (2 * j - 2 * side) % 128, 1)
+                old = narrow[side][i]
+                narrow[side][i] = moved if old is None else jnp.where(pair == j, moved, old)
+    for i in range(4):
+        PER[i] = narrow[0][i]
+        PEL[i] = narrow[1][i]
 
     pl.semaphore_wait(barrier, 8)
     every = (pl.ds(0, 9),)
-    first = edge_copies(PO, PLX, PRX, pl.ds(0, 11))
-    first += row_copies(FL, every, 0, 2, True, True)
-    first = begin(first)
-    rows = begin(pop_rows(F, (pl.ds(0, 3),), 8))
+    lows, highs = pl.ds(0, 14), pl.ds(5, 14)
+    copies = edge_copies(PER, PAL, PAR, pl.ds(0, 4), PEL)
+    copies.append(remote(PAO.at[lows, pl.ds(10, 2)], PAO.at[lows, pl.ds(2, 2)], (xu, gy)))
+    copies.append(remote(PAO.at[highs, pl.ds(4, 2)], PAO.at[highs, pl.ds(12, 2)], (xd, gy)))
+    for copy in copies:
+        copy.start()
+    copies = edge_copies(PO, PLX, PRX, pl.ds(0, 2))
+    copies += row_copies(FL, every, 0, 2, True, True)
+    for copy in copies:
+        copy.start()
+    first = close()
+    rows2 = begin(pop_rows(F, (pl.ds(2, 1),), 8))
+    rows = begin(pop_rows(F, (pl.ds(0, 2),), 8))
 
     loads[3].wait()
     loads[4].wait()
-    saved(NE, DE, FE, 11)
+    saved(NE, DE, FE, 2)
     second_set = begin(
-        edge_copies(PO, PLX, PRX, pl.ds(11, 2)) + row_copies(FE, every, 0, 2, True, True)
+        edge_copies(PO, PLX, PRX, pl.ds(2, 2)) + row_copies(FE, every, 0, 2, True, True)
     )
 
     def potentials(ref, strips):
@@ -569,16 +602,23 @@
             store_strip(QS, f, fields[f])
 
     def all_thrusts(ref, strips):
+        def keep(k, t, get):
+            for s in range(3):
+                ratio = TAU[s] * SI[s, k] / get[s]
+                TB[18 + s, k] = ratio
+                for i in range(3):
+                    TB[3 * s + i, k] = t[3 * s + i]
+                    TB[9 + 3 * s + i, k] = get[3 + i] + ratio * t[3 * s + i]
+            TB[21, k] = 1.0 / (get[0] + get[1] + get[2])
+
         def body(k):
             rows = pl.ds(8 * k, 8)
-            t = thrusts(flat_loader(QM, k), [ref[6 + i, rows, :] for i in range(3)])
-            for f in range(9):
-                TB[f, k] = t[f]
+            get = [ref[f, rows, :] for f in range(9)]
+            keep(k, thrusts(flat_loader(QM, k), get[6:9]), get)
 
         over_tiles(body)
-        t = thrusts(strip_loader(QS), [strips[6 + i] for i in range(3)])
-        for f in range(9):
-            TB[f, 6] = t[f]
+        get = [strips[f] for f in range(9)]
+        keep(6, thrusts(strip_loader(QS), get[6:9]), get)
 
     def field_strips(ref, strips, tile0):
         for f in range(9):
@@ -591,40 +631,45 @@
                 slot,
             )
 
-    def adjoint_stage(ref, strips, main_moments, strip_moments):
-        def one(mom, k, rho, u, d, put_x, put_l):
-            psi = [SI[s, k] for s in range(3)]
-            t = [TB[f, k] for f in range(9)]
-            fields, m, dens = local_adjoint(mom, rho, u, psi, t, d)
-            for f in range(18):
-                put_x(f, fields[f])
-            for i in range(3):
-                put_l(i, m[i])
-                put_l(3 + i, dens[i])
-
+    def one(mom, k, get):
+        psi = [SI[s, k] for s in range(3)]
+        t = [TB[f, k] for f in range(22)]
+        return local_adjoint(
+            mom, get[0:3], get[3:6], psi, t[0:9], t[9:18], t[18:21], t[21]
+        )
+
+    def main_stage(ref, main_moments):
         def body(k):
             rows = pl.ds(8 * k, 8)
-
-            def put_x(f, v):
+            get = [ref[f, rows, :] for f in range(9)]
+            x, m, dens = one(main_moments(k), k, get)
+            for f, v in enumerate(x + products(x[6:9], get[6:9])):
                 XM[f, pl.ds(16 + 8 * k, 8), :] = v
                 XM[f, pl.ds(lax.rem(8 * k + 64, 96), 8), :] = v
-
-            def put_l(f, v):
+            for f, v in enumerate(m + dens):
                 LM[f, rows, :] = v
 
-            get = [ref[f, rows, :] for f in range(9)]
-            one(main_moments(k), k, get[0:3], get[3:6], get[6:9], put_x, put_l)
-
         over_tiles(body)
 
-        def put_x(f, v):
+    def strip_stage(strips, mom):
+        x, m, dens = one(mom, 6, [strips[f] for f in range(9)])
+        for f in range(9):
+            SX[f] = x[f]
+        for f, v in enumerate(m + dens):
+            LS[f, 8:16, :] = v
+
+    def close_strips(strips, own):
+        x = [SX[f] for f in range(9)]
+        if own:
+            inner = (c16 < 5) | (c16 >= 11)
+            for f in range(9):
+                v = own_strip(lambda z, h: XM[f, 16 + 12 * z + 4 * h : 24 + 12 * z + 4 * h, :], 0)
+                x[f] = jnp.where(inner, v, x[f])
+            for f in range(3, 6):
+                v = own_strip(lambda z, h: LM[f, 12 * z + 4 * h : 8 + 12 * z + 4 * h, :], 0)
+                LS[f, 8:16, :] = jnp.where(inner, v, LS[f, 8:16, :])
+        for f, v in enumerate(x + products(x[6:9], [strips[6 + i] for i in range(3)])):
             store_strip(XS, f, v)
-
-        def put_l(f, v):
-            LS[f, 8:16, :] = v
-
-        get = [strips[f] for f in range(9)]
-        one(strip_moments(), 6, get[0:3], get[3:6], get[6:9], put_x, put_l)
 
     def spread_stage(ref, strips):
         def body(k):
@@ -653,31 +698,68 @@
         high = pltpu.roll(ref[f, 6:14, :], 112, 1)
         return jnp.where(sub < 4, low, high)
 
-    def with_edges(v, edge, z):
+    def with_edges(v, edge, z, width=1):
         right = pltpu.roll(edge, (122 - 32 * z) % 128, 1)
         left = pltpu.roll(edge, (-32 * z - 10) % 128, 1)
-        return jnp.where(lane >= 126, right, jnp.where(lane < 2, left, v))
+        return jnp.where(lane >= 128 - width, right, jnp.where(lane < width, left, v))
 
     arrive(first)
-    field_strips(FL, SL, 9)
+    field_strips(FL, SL, 0)
     potentials(FL, SL)
     all_thrusts(FL, SL)
-    arrive(rows)
+
+    hsel, csel = group4 % 2 == 1, lane % 4 < 2
+    lefts, rights = {}, {}
+    for o, q in enumerate(ORDER):
+        cx, cy, _ = VELOCITY[q]
+        m = jnp.where(hsel, PAO[o, 6 + cx : 14 + cx, :], PAO[o, 2 + cx : 10 + cx, :])
+
+        def received(ref, group, place):
+            i, j = divmod(group.index(o), 4)
+            low = pltpu.roll(ref[i, 2 + cx : 10 + cx, :], (place - 2 * j) % 128, 1)
+            high = pltpu.roll(ref[i, 6 + cx : 14 + cx, :], (place + 4 - 2 * j) % 128, 1)
+            return jnp.where(hsel, high, low)
+
+        l = jnp.where(csel, received(PAL, RIGHTWARD, 0), m) if cy <= 0 else m
+        r = jnp.where(csel, m, received(PAR, LEFTWARD, 2)) if cy >= 0 else m
+        lefts[q] = shift_y(l, cy)
+        rights[q] = shift_y(r, cy)
+    lefts, rights = moments_of(lefts), moments_of(rights)
+
+    def expanded(l, r, s):
+        l = jnp.where(odd, pltpu.roll(l, (20 - 8 * s) % 128, 1), pltpu.roll(l, (8 - 8 * s) % 128, 1))
+        r = jnp.where(odd, pltpu.roll(r, (16 - 8 * s) % 128, 1), pltpu.roll(r, (4 - 8 * s) % 128, 1))
+        return jnp.where(c16 >= 8, l, r)
+
+    strip_stage(
+        SL,
+        [
+            (
+                expanded(lefts[0], rights[0], s),
+                [expanded(lefts[1][i], rights[1][i], s) for i in range(3)],
+                {key: expanded(lefts[2][key], rights[2][key], s) for key in lefts[2]},
+            )
+            for s in range(3)
+        ],
+    )
+    arrive(rows2)
 
     acc = [None] * 3
     for o, q in enumerate(ORDER):
         cx, cy, cz = VELOCITY[q]
-        tile, slot = 6 + o // 8, o % 8
+        slot = o % 8
         for z in range(4):
             v = shift_y(F[2, o, 8 + 12 * z + 2 + cx : 8 + 12 * z + 10 + cx, :], cy)
             if cy == -1:
+                i, j = divmod(RIGHTWARD.index(o), 4)
                 halo = pltpu.roll(
-                    PLX[tile, 4 + cx : 12 + cx, :], (-(32 * z + 4 * slot + 1)) % 128, 1
+                    PAL[i, 4 + cx : 12 + cx, :], (-(32 * z + 17 + 2 * j)) % 128, 1
                 )
                 v = jnp.where(lane == 0, halo, v)
             if cy == 1:
+                i, j = divmod(LEFTWARD.index(o), 4)
                 halo = pltpu.roll(
-                    PRX[tile, 4 + cx : 12 + cx, :], (127 - (32 * z + 4 * slot + 2)) % 128, 1
+                    PAR[i, 4 + cx : 12 + cx, :], (127 - (32 * z + 16 + 2 * j)) % 128, 1
                 )
                 v = jnp.where(lane == 127, halo, v)
             to = (z - cz) % 4
@@ -691,22 +773,6 @@
         + row_copies(FG, (pl.ds(5, 14),), 8, 2, False, True)
     )
 
-    def pop_strips(s, carry):
-        for o, q in enumerate(ORDER):
-            cx, cy, _ = VELOCITY[q]
-            SA[19 * s + o] = strip_of(
-                lambda z, h: F[
-                    s, o, 8 + 12 * z + 4 * h + cx : 8 + 12 * z + 4 * h + cx + 8, :
-                ],
-                cy,
-                lambda h: PLX[3 * s + o // 8, 2 + 4 * h + cx : 10 + 4 * h + cx, :],
-                lambda h: PRX[3 * s + o // 8, 2 + 4 * h + cx : 10 + 4 * h + cx, :],
-                o % 8,
-            )
-        return carry
-
-    lax.fori_loop(0, 3, pop_strips, 0)
-
     def pulled_moments(k):
         out = []
         for s in range(3):
@@ -717,17 +783,16 @@
             out.append(moments_of(g))
         return out
 
-    def pulled_strip_moments():
-        return [moments_of({q: SA[19 * s + SLOT[q]] for q in range(19)}) for s in range(3)]
-
-    adjoint_stage(FL, SL, pulled_moments, pulled_strip_moments)
+    arrive(rows)
+    main_stage(FL, pulled_moments)
+    close_strips(SL, True)
     spread_stage(FL, SL)
 
     acc = None
     for f in range(6):
         edge = folded(LS, f)
         for z in range(4):
-            v = with_edges(LM[f, 12 * z + 2 : 12 * z + 10, :], edge, z)
+            v = with_edges(LM[f, 12 * z + 2 : 12 * z + 10, :], edge, z, 1 + f // 3)
             FM[f, 16 + 12 * z + 2 : 16 + 12 * z + 10, :] = v
             acc = pack(acc, v, z, f)
     PMO[0] = acc
@@ -737,7 +802,7 @@
     )
 
     arrive(second_set)
-    field_strips(FE, SE, 11)
+    field_strips(FE, SE, 2)
     potentials(FE, SE)
     all_thrusts(FE, SE)
 
@@ -751,6 +816,22 @@
             lambda h: PGR[o // 8, 2 + 4 * h + cx : 10 + 4 * h + cx, :],
             o % 8,
         )
+
+
+    def keep_moments(k, g):
+        a, b, c = moments_of(g)
+        for f, v in enumerate([a, *b, *(c[key] for key in KEYS)]):
+            EX[f, k] = 0.2 * v
+
+    def kept_tile(k):
+        g = {}
+        for o, q in enumerate(ORDER):
+            cx, cy, _ = VELOCITY[q]
+            g[q] = shift_y(FG[o, pl.ds(8 * k + (8 + cx), 8), :], cy)
+        keep_moments(k, g)
+
+    over_tiles(kept_tile)
+    keep_moments(6, {q: SG[SLOT[q]] for q in range(19)})
 
     arrive(middle)
     for f in range(6):
@@ -769,16 +850,14 @@
         )
 
     def middle_moments(k):
-        g = {}
-        for o, q in enumerate(ORDER):
-            cx, cy, _ = VELOCITY[q]
-            g[q] = shift_y(FG[o, pl.ds(8 * k + (8 + cx), 8), :], cy)
-        return late_moments(flat_loader(FM, k), g)
+        return late_moments(flat_loader(FM, k), [EX[f, k] for f in range(10)])
 
     def middle_strip_moments():
-        return late_moments(strip_loader(MS), {q: SG[SLOT[q]] for q in range(19)})
-
-    adjoint_stage(FE, SE, middle_moments, middle_strip_moments)
+        return late_moments(strip_loader(MS), [EX[f, 6] for f in range(10)])
+
+    main_stage(FE, middle_moments)
+    strip_stage(SE, middle_strip_moments())
+    close_strips(SE, False)
     spread_stage(FE, SE)
 
     strip = strip_loader(MS)
@@ -791,7 +870,7 @@
     edges = [folded(LS, f) for f in range(6)]
     for z in range(4):
         for f in range(6):
-            FIN[f, z] = with_edges(LM[f, 12 * z + 2 : 12 * z + 10, :], edges[f], z)
+            FIN[f, z] = with_edges(LM[f, 12 * z + 2 : 12 * z + 10, :], edges[f], z, 1 + f // 3)
         for o, q in enumerate(ORDER):
             cx, cy, cz = VELOCITY[q]
             row = 12 * z + 2 + cx
@@ -837,22 +916,28 @@
         vmem(9, 48, 128),
         vmem(6, 80, 128),
         vmem(19, 64, 128),
-        vmem(13, 8, 128),
-        vmem(13, 16, 128),
-        vmem(13, 16, 128),
+        vmem(4, 8, 128),
+        vmem(4, 16, 128),
+        vmem(4, 16, 128),
+        vmem(19, 16, 128),
+        vmem(4, 8, 128),
+        vmem(4, 8, 128),
+        vmem(4, 16, 128),
+        vmem(4, 16, 128),
         vmem(3, 8, 128),
         vmem(3, 16, 128),
         vmem(3, 16, 128),
         vmem(1, 8, 128),
         vmem(1, 16, 128),
         vmem(1, 16, 128),
-        vmem(57, 8, 128),
+        vmem(9, 8, 128),
         vmem(19, 8, 128),
         vmem(9, 8, 128),
         vmem(9, 8, 128),
         vmem(6, 96, 128),
         vmem(6, 3, 24, 128),
-        vmem(9, 7, 8, 128),
+        vmem(22, 7, 8, 128),
+        vmem(10, 7, 8, 128),
         vmem(3, 7, 8, 128),
         vmem(18, 96, 128),
         vmem(18, 3, 24, 128),

time: 26.8 us -> 25.2 us (0.940)
  Pallas kernels: 26.7 us -> 25.1 us
    pallas_call x1, Pallas kernels: 25.7 us -> 24.1 us  [block(): pl.pallas_call(lambda *refs: kernel(size_x, size_y, *refs), out_shape=jax...]
where the time goes in v3:
time: 25.2 us; the launch traced here: 25.1 us
  Pallas kernels  25.1 us (100%)
    pallas_call x1, Pallas kernels, block(): pl.pallas_call(lambda *refs: kernel(size_x, size_y, *refs), out_shape=jax...  24.1 us
    pallas_call x1, Pallas kernels, block(): pl.pallas_call(expand, out_shape=jax.ShapeDtypeStruct((57, 4, 8, 128), F3...  0.99 us

profile of v3, /device:TPU:1, one launch (start us, length us, event | category | flops | bytes accessed | tf_op | source)
XLA Modules:
  0.0 25.1 jit_solution(13775788490032691747)
XLA Ops:
  0.0 24.1 %lattice_adjoint.1.fin = f32[25,4,8,128]{3,2,1,0:T(8,128)S(1)} custom-call(f32[57,4,8,128]{3,2,1,0:T(8,128)} %refs_0_.1, bf16[57,4,8,128]{3,2,1,0:T(8,128)(2,1)} %refs_1_.1, bf16[57,4,8,128]{3,2,1,0:T(8,128)(2,1)} %refs_2_.1, bf16[3,4,8,128]{3,2,1,0:T(8,128)(2,1)} %refs_3_.1, bf16[3,4,8,128]{3,2,1,0:T(8,128)(2,1)} %refs_4_.1), custom_call_target="tpu_custom_call" | custom-call | tf_op jit(solution)/shard_map/lattice_adjoint/pallas_call | solution.py:953
  24.1 1.0 %lattice_expand.1 = f32[57,4,8,128]{3,2,1,0:T(8,128)} custom-call(f32[25,4,8,128]{3,2,1,0:T(8,128)S(1)} %lattice_adjoint.1.fin), custom_call_target="tpu_custom_call" | custom-call | tf_op jit(solution)/shard_map/lattice_expand/pallas_call | solution.py:964

commit v4 on v3

--- a/solution.py
+++ b/solution.py
@@ -36,7 +36,7 @@
 RIGHTWARD = tuple(o for o, q in enumerate(ORDER) if VELOCITY[q][1] <= 0)
 LEFTWARD = tuple(o for o, q in enumerate(ORDER) if VELOCITY[q][1] >= 0)
 F32 = jnp.float32
-N_SETS = 6
+N_SETS = 8
 
 
 def up_y(v):
@@ -565,11 +565,8 @@
     copies.append(remote(PAO.at[highs, pl.ds(4, 2)], PAO.at[highs, pl.ds(12, 2)], (xd, gy)))
     for copy in copies:
         copy.start()
-    copies = edge_copies(PO, PLX, PRX, pl.ds(0, 2))
-    copies += row_copies(FL, every, 0, 2, True, True)
-    for copy in copies:
-        copy.start()
-    first = close()
+    first = begin(edge_copies(PO, PLX, PRX, pl.ds(0, 2)))
+    state_rows = begin(row_copies(FL, every, 0, 2, True, True))
     rows2 = begin(pop_rows(F, (pl.ds(2, 1),), 8))
     rows = begin(pop_rows(F, (pl.ds(0, 2),), 8))
 
@@ -580,7 +577,7 @@
         edge_copies(PO, PLX, PRX, pl.ds(2, 2)) + row_copies(FE, every, 0, 2, True, True)
     )
 
-    def potentials(ref, strips):
+    def potentials(ref):
         def body(k):
             rows = pl.ds(8 * k, 8)
             psi, fields = pick_potentials(
@@ -593,6 +590,8 @@
                 QM[f, pl.ds(lax.rem(8 * k + 64, 96), 8), :] = fields[f]
 
         over_tiles(body)
+
+    def strip_potentials(strips):
         psi, fields = pick_potentials(
             [strips[s] for s in range(3)], [strips[6 + i] for i in range(3)]
         )
@@ -601,22 +600,24 @@
         for f in range(6):
             store_strip(QS, f, fields[f])
 
-    def all_thrusts(ref, strips):
-        def keep(k, t, get):
-            for s in range(3):
-                ratio = TAU[s] * SI[s, k] / get[s]
-                TB[18 + s, k] = ratio
-                for i in range(3):
-                    TB[3 * s + i, k] = t[3 * s + i]
-                    TB[9 + 3 * s + i, k] = get[3 + i] + ratio * t[3 * s + i]
-            TB[21, k] = 1.0 / (get[0] + get[1] + get[2])
-
+    def keep(k, t, get):
+        for s in range(3):
+            ratio = TAU[s] * SI[s, k] / get[s]
+            TB[18 + s, k] = ratio
+            for i in range(3):
+                TB[3 * s + i, k] = t[3 * s + i]
+                TB[9 + 3 * s + i, k] = get[3 + i] + ratio * t[3 * s + i]
+        TB[21, k] = 1.0 / (get[0] + get[1] + get[2])
+
+    def main_thrusts(ref):
         def body(k):
             rows = pl.ds(8 * k, 8)
             get = [ref[f, rows, :] for f in range(9)]
             keep(k, thrusts(flat_loader(QM, k), get[6:9]), get)
 
         over_tiles(body)
+
+    def strip_thrusts(strips):
         get = [strips[f] for f in range(9)]
         keep(6, thrusts(strip_loader(QS), get[6:9]), get)
 
@@ -671,7 +672,7 @@
         for f, v in enumerate(x + products(x[6:9], [strips[6 + i] for i in range(3)])):
             store_strip(XS, f, v)
 
-    def spread_stage(ref, strips):
+    def main_spread(ref):
         def body(k):
             rows = pl.ds(8 * k, 8)
             new = spread(
@@ -684,6 +685,8 @@
                 LM[3 + s, rows, :] = new[s]
 
         over_tiles(body)
+
+    def strip_spread(strips):
         new = spread(
             strip_loader(XS),
             [LS[3 + s, 8:16, :] for s in range(3)],
@@ -703,10 +706,13 @@
         left = pltpu.roll(edge, (-32 * z - 10) % 128, 1)
         return jnp.where(lane >= 128 - width, right, jnp.where(lane < width, left, v))
 
+    arrive(state_rows)
+    potentials(FL)
+    main_thrusts(FL)
     arrive(first)
     field_strips(FL, SL, 0)
-    potentials(FL, SL)
-    all_thrusts(FL, SL)
+    strip_potentials(SL)
+    strip_thrusts(SL)
 
     hsel, csel = group4 % 2 == 1, lane % 4 < 2
     lefts, rights = {}, {}
@@ -786,7 +792,8 @@
     arrive(rows)
     main_stage(FL, pulled_moments)
     close_strips(SL, True)
-    spread_stage(FL, SL)
+    main_spread(FL)
+    strip_spread(SL)
 
     acc = None
     for f in range(6):
@@ -796,15 +803,15 @@
             FM[f, 16 + 12 * z + 2 : 16 + 12 * z + 10, :] = v
             acc = pack(acc, v, z, f)
     PMO[0] = acc
-    middle = begin(
-        edge_copies(PMO, PML, PMR, pl.ds(0, 1))
-        + row_copies(FM, (pl.ds(0, 6),), 16, 2, True, True)
-    )
+    middle_edges = begin(edge_copies(PMO, PML, PMR, pl.ds(0, 1)))
+    middle_rows = begin(row_copies(FM, (pl.ds(0, 6),), 16, 2, True, True))
 
     arrive(second_set)
+    potentials(FE)
+    main_thrusts(FE)
     field_strips(FE, SE, 2)
-    potentials(FE, SE)
-    all_thrusts(FE, SE)
+    strip_potentials(SE)
+    strip_thrusts(SE)
 
     arrive(kept)
     for o, q in enumerate(ORDER):
@@ -833,10 +840,29 @@
     over_tiles(kept_tile)
     keep_moments(6, {q: SG[SLOT[q]] for q in range(19)})
 
-    arrive(middle)
+    arrive(middle_rows)
     for f in range(6):
         FM[f, 0:16, :] = FM[f, 48:64, :]
         FM[f, 64:80, :] = FM[f, 16:32, :]
+
+    def middle_moments(k):
+        return late_moments(flat_loader(FM, k), [EX[f, k] for f in range(10)])
+
+    def middle_strip_moments():
+        return late_moments(strip_loader(MS), [EX[f, 6] for f in range(10)])
+
+    main_stage(FE, middle_moments)
+    main_spread(FE)
+    for z in range(4):
+        for o, q in enumerate(ORDER):
+            cx, cy, cz = VELOCITY[q]
+            row = 12 * z + 2 + cx
+            mid = [FM[i, 16 + row + 12 * cz : 24 + row + 12 * cz, :] for i in (0, 1, 2, 5)]
+            v = plus(mid[3], along(q, mid[0:3])) + 0.2 * FG[o, 8 + row : 16 + row, :]
+            FIN[6 + q, z] = 0.2 * shift_y(v, cy)
+
+    arrive(middle_edges)
+    for f in range(6):
         store_strip(
             MS,
             f,
@@ -848,38 +874,23 @@
                 f,
             ),
         )
-
-    def middle_moments(k):
-        return late_moments(flat_loader(FM, k), [EX[f, k] for f in range(10)])
-
-    def middle_strip_moments():
-        return late_moments(strip_loader(MS), [EX[f, 6] for f in range(10)])
-
-    main_stage(FE, middle_moments)
     strip_stage(SE, middle_strip_moments())
     close_strips(SE, False)
-    spread_stage(FE, SE)
+    strip_spread(SE)
 
     strip = strip_loader(MS)
     for o, q in enumerate(ORDER):
         cx, cy, cz = VELOCITY[q]
         if cy != 0:
             v = plus(strip(5, cx, cz), along(q, [strip(i, cx, cz) for i in range(3)]))
-            TS[o, 8:16, :] = shift_y(v, cy) + 0.2 * SG[o]
-
-    edges = [folded(LS, f) for f in range(6)]
-    for z in range(4):
-        for f in range(6):
-            FIN[f, z] = with_edges(LM[f, 12 * z + 2 : 12 * z + 10, :], edges[f], z, 1 + f // 3)
-        for o, q in enumerate(ORDER):
-            cx, cy, cz = VELOCITY[q]
-            row = 12 * z + 2 + cx
-            mid = [FM[i, 16 + row + 12 * cz : 24 + row + 12 * cz, :] for i in (0, 1, 2, 5)]
-            v = plus(mid[3], along(q, mid[0:3])) + 0.2 * FG[o, 8 + row : 16 + row, :]
-            v = shift_y(v, cy)
-            if cy != 0:
-                v = with_edges(v, folded(TS, o), z)
-            FIN[6 + q, z] = 0.2 * v
+            TS[o, 8:16, :] = 0.2 * (shift_y(v, cy) + 0.2 * SG[o])
+            edge = folded(TS, o)
+            for z in range(4):
+                FIN[6 + q, z] = with_edges(FIN[6 + q, z], edge, z)
+    for f in range(6):
+        edge = folded(LS, f)
+        for z in range(4):
+            FIN[f, z] = with_edges(LM[f, 12 * z + 2 : 12 * z + 10, :], edge, z, 1 + f // 3)
 
     wait_rows(sum(sent), ssem.at[0])
 

time: 25.2 us -> 25.2 us (level)
  no operation moved by 1% of the time
where the time goes in v4:
time: 25.2 us; the launch traced here: 25.1 us
  Pallas kernels  25 us (99%)
    pallas_call x1, Pallas kernels, block(): pl.pallas_call(lambda *refs: kernel(size_x, size_y, *refs), out_shape=jax...  24.1 us
    pallas_call x1, Pallas kernels, block(): pl.pallas_call(expand, out_shape=jax.ShapeDtypeStruct((57, 4, 8, 128), F3...  0.99 us

profile of v4, /device:TPU:1, one launch (start us, length us, event | category | flops | bytes accessed | tf_op | source)
XLA Modules:
  0.0 25.1 jit_solution(17272968667765528103)
XLA Ops:
  0.0 24.1 %lattice_adjoint.1.fin = f32[25,4,8,128]{3,2,1,0:T(8,128)S(1)} custom-call(f32[57,4,8,128]{3,2,1,0:T(8,128)} %refs_0_.1, bf16[57,4,8,128]{3,2,1,0:T(8,128)(2,1)} %refs_1_.1, bf16[57,4,8,128]{3,2,1,0:T(8,128)(2,1)} %refs_2_.1, bf16[3,4,8,128]{3,2,1,0:T(8,128)(2,1)} %refs_3_.1, bf16[3,4,8,128]{3,2,1,0:T(8,128)(2,1)} %refs_4_.1), custom_call_target="tpu_custom_call" | custom-call | tf_op jit(solution)/shard_map/lattice_adjoint/pallas_call | solution.py:964
  24.1 1.0 %lattice_expand.1 = f32[57,4,8,128]{3,2,1,0:T(8,128)} custom-call(f32[25,4,8,128]{3,2,1,0:T(8,128)S(1)} %lattice_adjoint.1.fin), custom_call_target="tpu_custom_call" | custom-call | tf_op jit(solution)/shard_map/lattice_expand/pallas_call | solution.py:975
